TPU v7x, 32 devices: a whole 2x2x4 slice. The times are simulated.
32 devices in a mesh: ray: 4 (over z), cell: 8 (over y, x, core).
Axes of the slice: x: 2, y: 2, z: 4, core: 2. Of those that a mesh axis runs over, the one named last changes fastest.
Arguments:
- right_side: float32 [8, 8192], P(None, 'ray'), may hold values from -6 to 6
- tiles: bfloat16 [32, 32, 256, 256], P('ray', 'cell'), may hold values from -0.375 to 0.375
- pattern: int32 [32, 32], P('ray', 'cell'), may hold values from 0 to 31, as said below
- counts: int32 [32, 8], P('ray', 'cell'), may hold values from 1 to 4, as said below
Outputs:
- solution: float32 [8, 65536], P(None, 'cell')
- misfit: float32 [8], replicated
Inputs may be any that keep to these rules, and one draw needn't show every extreme that they name: `pattern`: each entry indexes a block within the slot's group of 32 cell blocks; a bundle may name a block more than once. Ragged counts; some bundle has all 4 slots live in some group, and some has one.
All inputs are finite; a program needn't handle non-finite values.
Results may differ from a plain program's by a relative error of at most 0.0014.
Values may be sent and summed in bfloat16 or wider, within the bound.
A program may use at most 64 MiB of HBM per device.

v0:
```python
import jax
import jax.numpy as jnp
from jax import lax
from jax.sharding import PartitionSpec as P

BLK_DEV = 32
ITERS = 4


def norm_rows(local_sq):
    total = lax.psum(local_sq, "ray")
    return jnp.sqrt(total + 1e-06)


def norm_cols(local_sq):
    total = lax.psum(local_sq, "cell")
    return jnp.sqrt(total + 1e-06)


def local(right_side, tiles, pattern, counts):
    nrhs = right_side.shape[0]
    bundles = tiles.shape[0]
    slots = tiles.shape[1]
    ray_rows = tiles.shape[2]
    block_cells = tiles.shape[3]
    blocks = BLK_DEV
    live = lax.broadcasted_iota(jnp.int32, pattern.shape, 1) < counts
    live_bf = live.astype(jnp.bfloat16)
    selector = (
        (pattern[:, :, None] == lax.broadcasted_iota(jnp.int32, (bundles, slots, blocks), 2))
        & live[:, :, None]
    ).astype(jnp.float32)

    def adjoint(vector_bf):
        rows = vector_bf.reshape(nrhs, bundles, ray_rows)
        per = jnp.einsum("bsrc,nbr->bsnc", tiles, rows, preferred_element_type=jnp.float32)
        total = jnp.einsum("bsk,bsnc->nkc", selector, per, precision=lax.Precision.HIGHEST)
        return total.reshape(nrhs, blocks * block_cells)

    u_state = right_side
    beta = norm_rows(jnp.sum(u_state * u_state, axis=1))
    u_state = u_state / beta[:, None]

    def rows_bf(state):
        return state.astype(jnp.bfloat16)

    def cols_reduce(adj_terms):
        return lax.psum(adj_terms, "ray")

    v_state = cols_reduce(adjoint(rows_bf(u_state)))
    alpha = norm_cols(jnp.sum(v_state * v_state, axis=1))
    v_state = v_state / alpha[:, None]
    w_state = v_state
    x_state = jnp.zeros_like(v_state)
    phibar = beta
    rhobar = alpha
    for step in range(ITERS):
        vblocks = v_state.astype(jnp.bfloat16).reshape(nrhs, blocks, block_cells)
        picked = vblocks[:, pattern] * live_bf[None, :, :, None]
        partial_value = jnp.einsum(
            "bsrc,nbsc->nbr", tiles, picked, preferred_element_type=jnp.float32
        )
        partial_value = partial_value.reshape(nrhs, bundles * ray_rows)
        summed = lax.psum(partial_value, "cell")
        u_state = summed - alpha[:, None] * u_state
        beta = norm_rows(jnp.sum(u_state * u_state, axis=1))
        u_state = u_state / beta[:, None]
        v_state = cols_reduce(adjoint(rows_bf(u_state))) - beta[:, None] * v_state
        alpha = norm_cols(jnp.sum(v_state * v_state, axis=1))
        v_state = v_state / alpha[:, None]
        rho = jnp.sqrt(rhobar * rhobar + beta * beta)
        cosine = rhobar / rho
        sine = beta / rho
        theta = sine * alpha
        rhobar = -cosine * alpha
        phi = cosine * phibar
        phibar = sine * phibar
        x_state = x_state + (phi / rho)[:, None] * w_state
        w_state = v_state - (theta / rho)[:, None] * w_state
    return (x_state, phibar)


def solution(mesh):
    in_specs = (P(None, "ray"), P("ray", "cell", None, None), P("ray", "cell"), P("ray", "cell"))
    out_specs = (P(None, "cell"), P())
    return jax.shard_map(local, mesh=mesh, in_specs=in_specs, out_specs=out_specs, check_vma=False)
```

profile of v0, /device:TPU:0, one launch (start us, length us, event | category | flops | bytes accessed | tf_op | source)
XLA Modules:
  0.0 515.1 jit_solution(9101913132747717034)
XLA Ops:
  8.2 13.5 %psum.119 = f32[8]{0:T(128)S(1)} all-reduce(f32[8]{0:T(128)S(1)} %multiply_reduce_fusion.8), channel_id=1, replica_groups=mesh['ray'=4,'cell'=8] {'ray'}, use_global_device_ids=true, to_apply=%region_1.0 | all-reduce | flops 8 | bytes 64 | tf_op jit(solution)/shard_map/psum | solution.py:11
  23.4 2.8 fusion.51
  27.9 33.7 %all-reduce.9.cloned.1.call-done = f32[8,8192]{1,0:T(8,128)} async-done(((f32[8,8192]{1,0:T(8,128)}), f32[8,8192]{1,0:T(8,128)}) %all-reduce.9.cloned.1.call-update) | async-done | bytes 262160 | tf_op jit(solution)/shard_map/psum | solution.py:48
  61.6 1.1 multiply_reduce_fusion.3
  62.7 11.8 %psum.121 = f32[8]{0:T(128)S(1)} all-reduce(f32[8]{0:T(128)S(1)} %multiply_reduce_fusion.3), channel_id=1, replica_groups=mesh['ray'=4,'cell'=8] {'cell'}, use_global_device_ids=true, to_apply=%region_4.0 | all-reduce | flops 8 | bytes 64 | tf_op jit(solution)/shard_map/psum | solution.py:16
  76.2 4.1 fusion.14
  80.3 52.3 %all-reduce.11.cloned.1.call-done = f32[8,2048]{1,0:T(8,128)} async-done(((f32[8,2048]{1,0:T(8,128)}), f32[8,2048]{1,0:T(8,128)}) %all-reduce.11.cloned.1.call-update) | async-done | bytes 65552 | tf_op jit(solution)/shard_map/psum | solution.py:64
  133.6 11.7 %psum.123 = f32[8]{0:T(128)S(1)} all-reduce(f32[8]{0:T(128)S(1)} %get-tuple-element.21), channel_id=1, replica_groups=mesh['ray'=4,'cell'=8] {'ray'}, use_global_device_ids=true, to_apply=%region_7.0 | all-reduce | flops 8 | bytes 64 | tf_op jit(solution)/shard_map/psum | solution.py:11
  145.4 2.8 fusion.52
  149.7 32.3 %all-reduce.13.cloned.1.call-done = f32[8,8192]{1,0:T(8,128)} async-done(((f32[8,8192]{1,0:T(8,128)}), f32[8,8192]{1,0:T(8,128)}) %all-reduce.13.cloned.1.call-update) | async-done | bytes 262160 | tf_op jit(solution)/shard_map/psum | solution.py:48
  182.0 1.2 multiply_reduce_fusion.2
  183.2 11.8 %psum.125 = f32[8]{0:T(128)S(1)} all-reduce(f32[8]{0:T(128)S(1)} %multiply_reduce_fusion.2), channel_id=1, replica_groups=mesh['ray'=4,'cell'=8] {'cell'}, use_global_device_ids=true, to_apply=%region_10.0 | all-reduce | flops 8 | bytes 64 | tf_op jit(solution)/shard_map/psum | solution.py:16
  195.0 1.1 fusion.50
  196.7 4.0 fusion.12
  200.8 52.3 %all-reduce.15.cloned.1.call-done = f32[8,2048]{1,0:T(8,128)} async-done(((f32[8,2048]{1,0:T(8,128)}), f32[8,2048]{1,0:T(8,128)}) %all-reduce.15.cloned.1.call-update) | async-done | bytes 65552 | tf_op jit(solution)/shard_map/psum | solution.py:64
  254.1 11.7 %psum.127 = f32[8]{0:T(128)S(1)} all-reduce(f32[8]{0:T(128)S(1)} %get-tuple-element.17), channel_id=1, replica_groups=mesh['ray'=4,'cell'=8] {'ray'}, use_global_device_ids=true, to_apply=%region_13.0 | all-reduce | flops 8 | bytes 64 | tf_op jit(solution)/shard_map/psum | solution.py:11
  265.9 2.8 fusion.53
  270.1 32.3 %all-reduce.17.cloned.1.call-done = f32[8,8192]{1,0:T(8,128)} async-done(((f32[8,8192]{1,0:T(8,128)}), f32[8,8192]{1,0:T(8,128)}) %all-reduce.17.cloned.1.call-update) | async-done | bytes 262160 | tf_op jit(solution)/shard_map/psum | solution.py:48
  302.4 1.2 multiply_reduce_fusion.1
  303.6 11.8 %psum.129 = f32[8]{0:T(128)S(1)} all-reduce(f32[8]{0:T(128)S(1)} %multiply_reduce_fusion.1), channel_id=1, replica_groups=mesh['ray'=4,'cell'=8] {'cell'}, use_global_device_ids=true, to_apply=%region_16.0 | all-reduce | flops 8 | bytes 64 | tf_op jit(solution)/shard_map/psum | solution.py:16
  315.4 1.1 fusion.49
  317.1 4.0 fusion.10
  321.2 52.3 %all-reduce.19.cloned.1.call-done = f32[8,2048]{1,0:T(8,128)} async-done(((f32[8,2048]{1,0:T(8,128)}), f32[8,2048]{1,0:T(8,128)}) %all-reduce.19.cloned.1.call-update) | async-done | bytes 65552 | tf_op jit(solution)/shard_map/psum | solution.py:64
  374.5 11.7 %psum.131 = f32[8]{0:T(128)S(1)} all-reduce(f32[8]{0:T(128)S(1)} %get-tuple-element.13), channel_id=1, replica_groups=mesh['ray'=4,'cell'=8] {'ray'}, use_global_device_ids=true, to_apply=%region_19.0 | all-reduce | flops 8 | bytes 64 | tf_op jit(solution)/shard_map/psum | solution.py:11
  386.3 2.8 fusion.54
  390.5 32.3 %all-reduce.21.cloned.1.call-done = f32[8,8192]{1,0:T(8,128)} async-done(((f32[8,8192]{1,0:T(8,128)}), f32[8,8192]{1,0:T(8,128)}) %all-reduce.21.cloned.1.call-update) | async-done | bytes 262160 | tf_op jit(solution)/shard_map/psum | solution.py:48
  422.8 1.3 multiply_reduce_fusion
  424.1 11.8 %psum.133 = f32[8]{0:T(128)S(1)} all-reduce(f32[8]{0:T(128)S(1)} %multiply_reduce_fusion), channel_id=1, replica_groups=mesh['ray'=4,'cell'=8] {'cell'}, use_global_device_ids=true, to_apply=%region_22.0 | all-reduce | flops 8 | bytes 64 | tf_op jit(solution)/shard_map/psum | solution.py:16
  435.9 1.1 fusion.24
  437.6 4.0 fusion.8
  441.6 52.3 %all-reduce.23.cloned.1.call-done = f32[8,2048]{1,0:T(8,128)} async-done(((f32[8,2048]{1,0:T(8,128)}), f32[8,2048]{1,0:T(8,128)}) %all-reduce.23.cloned.1.call-update) | async-done | bytes 65552 | tf_op jit(solution)/shard_map/psum | solution.py:64
  495.0 11.7 %psum.135 = f32[8]{0:T(128)S(1)} all-reduce(f32[8]{0:T(128)S(1)} %multiply_reduce_fusion.4), channel_id=1, replica_groups=mesh['ray'=4,'cell'=8] {'ray'}, use_global_device_ids=true, to_apply=%region_25.0 | all-reduce | flops 8 | bytes 64 | tf_op jit(solution)/shard_map/psum | solution.py:11
  (63 shorter events, 18.0 us)
Async XLA Ops:
  7.2 19.1 %copy-start.3 = (s32[8,4]{0,1:T(4,128)S(1)}, s32[8,4]{0,1:T(4,128)}, u32[]{:S(2)}) copy-start(s32[8,4]{0,1:T(4,128)} %param.6) | copy-start | bytes 388
  7.2 54.4 %all-reduce.9.cloned.1.call-start = ((), (), s32[]{:S(2)}) async-start(), calls=%async_computation | async-start | bytes 524288 | tf_op jit(solution)/shard_map/psum | solution.py:48
  26.3 106.3 %copy-start.2 = (f32[8,2048]{1,0:T(8,128)S(1)}, f32[8,2048]{1,0:T(8,128)}, u32[]{:S(2)}) copy-start(f32[8,2048]{1,0:T(8,128)} %param.4) | copy-start | bytes 196612
  27.6 105.0 %all-reduce.11.cloned.1.call-start = ((), (), s32[]{:S(2)}) async-start(), calls=%async_computation.1 | async-start | bytes 131072 | tf_op jit(solution)/shard_map/psum | solution.py:64
  76.2 105.8 %copy-start = (f32[8,8192]{1,0:T(8,128)S(1)}, f32[8,8192]{1,0:T(8,128)}, u32[]{:S(2)}) copy-start(f32[8,8192]{1,0:T(8,128)} %all-reduce.9.cloned.1.call-done) | copy-start | bytes 786436
  80.3 101.7 %all-reduce.13.cloned.1.call-start = ((), (), s32[]{:S(2)}) async-start(), calls=%async_computation.2 | async-start | bytes 524288 | tf_op jit(solution)/shard_map/psum | solution.py:48
  149.6 103.4 %all-reduce.15.cloned.1.call-start = ((), (), s32[]{:S(2)}) async-start(), calls=%async_computation.3 | async-start | bytes 131072 | tf_op jit(solution)/shard_map/psum | solution.py:64
  200.7 101.7 %all-reduce.17.cloned.1.call-start = ((), (), s32[]{:S(2)}) async-start(), calls=%async_computation.4 | async-start | bytes 524288 | tf_op jit(solution)/shard_map/psum | solution.py:48
  270.1 103.4 %all-reduce.19.cloned.1.call-start = ((), (), s32[]{:S(2)}) async-start(), calls=%async_computation.5 | async-start | bytes 131072 | tf_op jit(solution)/shard_map/psum | solution.py:64
  321.1 101.7 %all-reduce.21.cloned.1.call-start = ((), (), s32[]{:S(2)}) async-start(), calls=%async_computation.6 | async-start | bytes 524288 | tf_op jit(solution)/shard_map/psum | solution.py:48
  390.5 103.5 %all-reduce.23.cloned.1.call-start = ((), (), s32[]{:S(2)}) async-start(), calls=%async_computation.7 | async-start | bytes 131072 | tf_op jit(solution)/shard_map/psum | solution.py:64
  422.8 84.5 %copy-start.1 = (f32[8,8192]{1,0:T(8,128)S(1)}, f32[8,8192]{1,0:T(8,128)}, u32[]{:S(2)}) copy-start(f32[8,8192]{1,0:T(8,128)} %all-reduce.21.cloned.1.call-done) | copy-start | bytes 786436
Sparse Core Ops, SparseCore 0:
  27.7 33.7 all-reduce.8
  80.4 52.1 all-reduce.10
  149.7 32.1 all-reduce.12
  200.8 52.1 all-reduce.14
  270.2 32.1 all-reduce.16
  321.3 52.1 all-reduce.18
  390.6 32.1 all-reduce.20
  441.7 52.1 all-reduce.22
where the time goes:
time: 516 us; the launch traced here: 515 us
  waiting for transfers between devices  340 us (66%)
  blocking collectives  108 us (21%)
  matrix products  29.3 us (6%)
  other arithmetic  17.7 us (3%)
  between operations  14.3 us (3%)
  local copies, waits for them, and re-layouts  5.99 us (1%)
    psum x4, waiting for transfers between devices, local(): summed = lax.psum(partial_value, 'cell')  209 us
    psum x4, waiting for transfers between devices, cols_reduce(): return lax.psum(adj_terms, 'ray')  131 us
    psum x5, blocking collectives, norm_rows(): total = lax.psum(local_sq, 'ray')  60.2 us
    psum x4, blocking collectives, norm_cols(): total = lax.psum(local_sq, 'cell')  47.3 us
    dot_general x4, matrix products, local(): jnp.einsum('bsrc,nbsc->nbr', tiles, picked, preferred_element_type=jnp.fl...  16.1 us
    dot_general x4, matrix products, adjoint(): jnp.einsum('bsrc,nbr->bsnc', tiles, rows, preferred_element_type=jnp.floa...  11.4 us
  transfers between devices with their start and end apart: 8, of which 8 were waited for; matrix products, arithmetic and copies ran while one was open for 0% of the time, Pallas kernels for 0%

commit v1 on v0

--- a/solution.py
+++ b/solution.py
@@ -61,7 +61,7 @@
             "bsrc,nbsc->nbr", tiles, picked, preferred_element_type=jnp.float32
         )
         partial_value = partial_value.reshape(nrhs, bundles * ray_rows)
-        summed = lax.psum(partial_value, "cell")
+        summed = jnp.sum(lax.all_gather(partial_value, "cell"), axis=0)
         u_state = summed - alpha[:, None] * u_state
         beta = norm_rows(jnp.sum(u_state * u_state, axis=1))
         u_state = u_state / beta[:, None]

time: 516 us -> 337 us (0.65)
  waiting for transfers between devices: 340 us -> 132 us
  blocking collectives: 108 us -> 143 us
    psum x4 -> x0, waiting for transfers between devices: 209 us -> none  [local(): summed = lax.psum(partial_value, 'cell')]
    all_gather x0 -> x4, blocking collectives: none -> 39.4 us  [local(): summed = jnp.sum(lax.all_gather(partial_value, 'cell'), axis=0)]
  transfers between devices with their start and end apart: 8 -> 4, of which waited for: 8 -> 4; matrix products, arithmetic and copies ran while one was open for 0% -> 0% of each run, Pallas kernels for 0% -> 0%
where the time goes in v1:
time: 337 us; the launch traced here: 336 us
  blocking collectives  143 us (42%)
  waiting for transfers between devices  132 us (39%)
  matrix products  26.7 us (8%)
  other arithmetic  14.4 us (4%)
  between operations  13.9 us (4%)
  local copies, waits for them, and re-layouts  5.99 us (2%)
    psum x4, waiting for transfers between devices, cols_reduce(): return lax.psum(adj_terms, 'ray')  132 us
    psum x5, blocking collectives, norm_rows(): total = lax.psum(local_sq, 'ray')  56.1 us
    psum x4, blocking collectives, norm_cols(): total = lax.psum(local_sq, 'cell')  47.3 us
    all_gather x4, blocking collectives, local(): summed = jnp.sum(lax.all_gather(partial_value, 'cell'), axis=0)  39.4 us
    dot_general x4, matrix products, local(): jnp.einsum('bsrc,nbsc->nbr', tiles, picked, preferred_element_type=jnp.fl...  13.5 us
    dot_general x4, matrix products, adjoint(): jnp.einsum('bsrc,nbr->bsnc', tiles, rows, preferred_element_type=jnp.floa...  11.4 us
  transfers between devices with their start and end apart: 4, of which 4 were waited for; matrix products, arithmetic and copies ran while one was open for 0% of the time, Pallas kernels for 0%

profile of v1, /device:TPU:0, one launch (start us, length us, event | category | flops | bytes accessed | tf_op | source)
XLA Modules:
  0.0 336.2 jit_solution(2611223568040794773)
XLA Ops:
  8.2 13.5 %psum.91 = f32[8]{0:T(128)S(1)} all-reduce(f32[8]{0:T(128)S(1)} %multiply_reduce_fusion.8), channel_id=1, replica_groups=mesh['ray'=4,'cell'=8] {'ray'}, use_global_device_ids=true, to_apply=%region_1.0 | all-reduce | flops 8 | bytes 64 | tf_op jit(solution)/shard_map/psum | solution.py:11
  23.4 2.8 convolution_bitcast_fusion.7
  27.9 33.7 %all-reduce.5.cloned.1.call-done = f32[8,8192]{1,0:T(8,128)} async-done(((f32[8,8192]{1,0:T(8,128)}), f32[8,8192]{1,0:T(8,128)}) %all-reduce.5.cloned.1.call-update) | async-done | bytes 262160 | tf_op jit(solution)/shard_map/psum | solution.py:48
  61.6 1.1 multiply_reduce_fusion.3
  62.7 11.8 %psum.93 = f32[8]{0:T(128)S(1)} all-reduce(f32[8]{0:T(128)S(1)} %multiply_reduce_fusion.3), channel_id=1, replica_groups=mesh['ray'=4,'cell'=8] {'cell'}, use_global_device_ids=true, to_apply=%region_4.0 | all-reduce | flops 8 | bytes 64 | tf_op jit(solution)/shard_map/psum | solution.py:16
  76.2 3.4 %fusion.10 = f32[8,8,256,1]{2,1,3,0:T(8,128)S(1)} fusion(bf16[8,4,256,256]{3,2,1,0:T(8,128)(2,1)} %param.5, bf16[8,4,8,256]{3,2,1,0:T(8,128)(2,1)S(1)} %bitcast.124, bf16[8,4]{1,0:T(8,128)(2,1)S(1)} %get-tuple-element.30), kind=kOutput, calls=%fused_computation.30 | convolution fusion | flops 33619968 | bytes 4390976 | tf_op jit(solution)/shard_map/bsrc,nbsc->nbr/dot_general | solution.py:60
  79.5 9.9 %all_gather.12 = f32[8,8,2048]{2,1,0:T(8,128)S(1)} all-gather(f32[1,8,2048]{2,1,0:T(8,128)S(1)} %bitcast.132), channel_id=1, replica_groups=mesh['ray'=4,'cell'=8] {'cell'}, dimensions={0}, use_global_device_ids=true | all-gather | bytes 589824 | tf_op jit(solution)/shard_map/all_gather | solution.py:64
  89.7 10.7 %psum.94 = f32[8]{0:T(128)S(1)} all-reduce(f32[8]{0:T(128)S(1)} %get-tuple-element.21), channel_id=1, replica_groups=mesh['ray'=4,'cell'=8] {'ray'}, use_global_device_ids=true, to_apply=%region_7.0 | all-reduce | flops 8 | bytes 64 | tf_op jit(solution)/shard_map/psum | solution.py:11
  100.5 2.9 convolution_bitcast_fusion.6
  104.7 32.7 %all-reduce.7.cloned.1.call-done = f32[8,8192]{1,0:T(8,128)} async-done(((f32[8,8192]{1,0:T(8,128)}), f32[8,8192]{1,0:T(8,128)}) %all-reduce.7.cloned.1.call-update) | async-done | bytes 262160 | tf_op jit(solution)/shard_map/psum | solution.py:48
  137.5 1.2 multiply_reduce_fusion.2
  138.7 11.8 %psum.96 = f32[8]{0:T(128)S(1)} all-reduce(f32[8]{0:T(128)S(1)} %multiply_reduce_fusion.2), channel_id=1, replica_groups=mesh['ray'=4,'cell'=8] {'cell'}, use_global_device_ids=true, to_apply=%region_10.0 | all-reduce | flops 8 | bytes 64 | tf_op jit(solution)/shard_map/psum | solution.py:16
  150.5 1.1 fusion.46
  152.2 3.4 %fusion.8 = f32[8,8,256,1]{2,1,3,0:T(8,128)S(1)} fusion(bf16[8,4,256,256]{3,2,1,0:T(8,128)(2,1)} %param.5, bf16[8,4,8,256]{3,2,1,0:T(8,128)(2,1)S(1)} %bitcast.125, bf16[8,4]{1,0:T(8,128)(2,1)S(1)} %get-tuple-element.30), kind=kOutput, calls=%fused_computation.28 | convolution fusion | flops 33619968 | bytes 4390976 | tf_op jit(solution)/shard_map/bsrc,nbsc->nbr/dot_general | solution.py:60
  155.5 9.8 %all_gather.13 = f32[8,8,2048]{2,1,0:T(8,128)S(1)} all-gather(f32[1,8,2048]{2,1,0:T(8,128)S(1)} %bitcast.133), channel_id=1, replica_groups=mesh['ray'=4,'cell'=8] {'cell'}, dimensions={0}, use_global_device_ids=true | all-gather | bytes 589824 | tf_op jit(solution)/shard_map/all_gather | solution.py:64
  165.6 10.7 %psum.97 = f32[8]{0:T(128)S(1)} all-reduce(f32[8]{0:T(128)S(1)} %get-tuple-element.17), channel_id=1, replica_groups=mesh['ray'=4,'cell'=8] {'ray'}, use_global_device_ids=true, to_apply=%region_13.0 | all-reduce | flops 8 | bytes 64 | tf_op jit(solution)/shard_map/psum | solution.py:11
  176.3 2.9 convolution_bitcast_fusion.5
  180.6 32.7 %all-reduce.9.cloned.1.call-done = f32[8,8192]{1,0:T(8,128)} async-done(((f32[8,8192]{1,0:T(8,128)}), f32[8,8192]{1,0:T(8,128)}) %all-reduce.9.cloned.1.call-update) | async-done | bytes 262160 | tf_op jit(solution)/shard_map/psum | solution.py:48
  213.3 1.2 multiply_reduce_fusion.1
  214.5 11.8 %psum.99 = f32[8]{0:T(128)S(1)} all-reduce(f32[8]{0:T(128)S(1)} %multiply_reduce_fusion.1), channel_id=1, replica_groups=mesh['ray'=4,'cell'=8] {'cell'}, use_global_device_ids=true, to_apply=%region_16.0 | all-reduce | flops 8 | bytes 64 | tf_op jit(solution)/shard_map/psum | solution.py:16
  226.3 1.1 fusion.45
  228.0 3.4 %fusion.6 = f32[8,8,256,1]{2,1,3,0:T(8,128)S(1)} fusion(bf16[8,4,256,256]{3,2,1,0:T(8,128)(2,1)} %param.5, bf16[8,4,8,256]{3,2,1,0:T(8,128)(2,1)S(1)} %bitcast.126, bf16[8,4]{1,0:T(8,128)(2,1)S(1)} %get-tuple-element.30), kind=kOutput, calls=%fused_computation.26 | convolution fusion | flops 33619968 | bytes 4390976 | tf_op jit(solution)/shard_map/bsrc,nbsc->nbr/dot_general | solution.py:60
  231.4 9.8 %all_gather.14 = f32[8,8,2048]{2,1,0:T(8,128)S(1)} all-gather(f32[1,8,2048]{2,1,0:T(8,128)S(1)} %bitcast.134), channel_id=1, replica_groups=mesh['ray'=4,'cell'=8] {'cell'}, dimensions={0}, use_global_device_ids=true | all-gather | bytes 589824 | tf_op jit(solution)/shard_map/all_gather | solution.py:64
  241.4 10.7 %psum.100 = f32[8]{0:T(128)S(1)} all-reduce(f32[8]{0:T(128)S(1)} %get-tuple-element.13), channel_id=1, replica_groups=mesh['ray'=4,'cell'=8] {'ray'}, use_global_device_ids=true, to_apply=%region_19.0 | all-reduce | flops 8 | bytes 64 | tf_op jit(solution)/shard_map/psum | solution.py:11
  252.1 2.9 convolution_bitcast_fusion.4
  256.4 33.0 %all-reduce.11.cloned.1.call-done = f32[8,8192]{1,0:T(8,128)} async-done(((f32[8,8192]{1,0:T(8,128)}), f32[8,8192]{1,0:T(8,128)}) %all-reduce.11.cloned.1.call-update) | async-done | bytes 262160 | tf_op jit(solution)/shard_map/psum | solution.py:48
  289.3 1.3 multiply_reduce_fusion
  290.6 11.8 %psum.102 = f32[8]{0:T(128)S(1)} all-reduce(f32[8]{0:T(128)S(1)} %multiply_reduce_fusion), channel_id=1, replica_groups=mesh['ray'=4,'cell'=8] {'cell'}, use_global_device_ids=true, to_apply=%region_22.0 | all-reduce | flops 8 | bytes 64 | tf_op jit(solution)/shard_map/psum | solution.py:16
  302.4 1.1 fusion.20
  304.1 3.4 %fusion.4 = f32[8,8,256,1]{2,1,3,0:T(8,128)S(1)} fusion(bf16[8,4,256,256]{3,2,1,0:T(8,128)(2,1)} %param.5, bf16[8,4,8,256]{3,2,1,0:T(8,128)(2,1)S(1)} %bitcast.123, bf16[8,4]{1,0:T(8,128)(2,1)S(1)} %get-tuple-element.30), kind=kOutput, calls=%fused_computation.24 | convolution fusion | flops 33619968 | bytes 4390976 | tf_op jit(solution)/shard_map/bsrc,nbsc->nbr/dot_general | solution.py:60
  307.4 9.8 %all_gather.15 = f32[8,8,2048]{2,1,0:T(8,128)S(1)} all-gather(f32[1,8,2048]{2,1,0:T(8,128)S(1)} %bitcast.131), channel_id=1, replica_groups=mesh['ray'=4,'cell'=8] {'cell'}, dimensions={0}, use_global_device_ids=true | all-gather | bytes 589824 | tf_op jit(solution)/shard_map/all_gather | solution.py:64
  317.5 10.7 %psum.103 = f32[8]{0:T(128)S(1)} all-reduce(f32[8]{0:T(128)S(1)} %multiply_reduce_fusion.4), channel_id=1, replica_groups=mesh['ray'=4,'cell'=8] {'ray'}, use_global_device_ids=true, to_apply=%region_25.0 | all-reduce | flops 8 | bytes 64 | tf_op jit(solution)/shard_map/psum | solution.py:11
  (59 shorter events, 14.5 us)
Async XLA Ops:
  7.2 19.1 %copy-start.3 = (s32[8,4]{0,1:T(4,128)S(1)}, s32[8,4]{0,1:T(4,128)}, u32[]{:S(2)}) copy-start(s32[8,4]{0,1:T(4,128)} %param.6) | copy-start | bytes 388
  7.2 54.4 %all-reduce.5.cloned.1.call-start = ((), (), s32[]{:S(2)}) async-start(), calls=%async_computation | async-start | bytes 524288 | tf_op jit(solution)/shard_map/psum | solution.py:48
  26.3 63.3 %copy-start.2 = (f32[8,2048]{1,0:T(8,128)S(1)}, f32[8,2048]{1,0:T(8,128)}, u32[]{:S(2)}) copy-start(f32[8,2048]{1,0:T(8,128)} %param.4) | copy-start | bytes 196612
  27.6 109.8 %all-reduce.7.cloned.1.call-start = ((), (), s32[]{:S(2)}) async-start(), calls=%async_computation.1 | async-start | bytes 524288 | tf_op jit(solution)/shard_map/psum | solution.py:48
  79.5 57.9 %copy-start = (f32[8,8192]{1,0:T(8,128)S(1)}, f32[8,8192]{1,0:T(8,128)}, u32[]{:S(2)}) copy-start(f32[8,8192]{1,0:T(8,128)} %all-reduce.5.cloned.1.call-done) | copy-start | bytes 786436
  104.7 108.6 %all-reduce.9.cloned.1.call-start = ((), (), s32[]{:S(2)}) async-start(), calls=%async_computation.2 | async-start | bytes 524288 | tf_op jit(solution)/shard_map/psum | solution.py:48
  180.5 108.8 %all-reduce.11.cloned.1.call-start = ((), (), s32[]{:S(2)}) async-start(), calls=%async_computation.3 | async-start | bytes 524288 | tf_op jit(solution)/shard_map/psum | solution.py:48
  289.3 39.4 %copy-start.1 = (f32[8,8192]{1,0:T(8,128)S(1)}, f32[8,8192]{1,0:T(8,128)}, u32[]{:S(2)}) copy-start(f32[8,8192]{1,0:T(8,128)} %all-reduce.11.cloned.1.call-done) | copy-start | bytes 786436
Sparse Core Ops, SparseCore 0:
  27.7 33.7 all-reduce.4
  104.8 32.6 all-reduce.6
  180.6 32.6 all-reduce.8
  256.5 32.7 all-reduce.10
